TPU v7x, 128 devices: a whole 4x4x4 slice. The times are simulated.
128 devices in a mesh: tm: 8 (over z, core), space: 16 (over y, x).
Axes of the slice: x: 4, y: 4, z: 4, core: 2. Of those that a mesh axis runs over, the one named last changes fastest.
Arguments:
- noise: bfloat16 [32, 1024, 8192], P('tm', 'space'), may hold values from -4 to 4
- scale: float32 [32, 8192], P('tm'), may hold values from 0.55 to 1
- tiles: bfloat16 [32, 64, 3, 128, 128], P('tm', 'space'), may hold values from -0.375 to 0.375
- columns: int32 [32, 64, 3], P('tm', 'space'), may hold values from 0 to 63, as said below
Outputs:
- samples: bfloat16 [32, 1024, 8192], P('tm', 'space')
Inputs may be any that keep to these rules, and one draw needn't show every extreme that they name: `columns`: in every tile row r of a time step the 3 entries are different, and the first is r itself.
All inputs are finite; a program needn't handle non-finite values.
Results may differ from a plain program's by a relative error of at most 0.03.
Values may be sent and summed in bfloat16 or wider, within the bound.
No kernel may reach another device: no remote copies, remote signals or barrier semaphores. Data moves between devices by JAX's collectives and lax.ppermute only.
A program may use at most 128 MiB of HBM per device.

v0:
```python
import jax
import jax.numpy as jnp
from jax import lax
from jax.sharding import PartitionSpec as P


def shifted(shard, axis, by):
    devices = lax.axis_size(axis)
    pairs = [(i, i + by) for i in range(devices) if 0 <= i + by < devices]
    return lax.ppermute(shard, axis, pairs)


def on_device(noise, scale, tiles, columns):
    step_count = noise.shape[0]
    local_samples = noise.shape[1]
    node_count = noise.shape[2]
    tile_count = tiles.shape[2]
    tile_size = tiles.shape[3]
    tile_rows = node_count // tile_size
    part_count = lax.axis_size("tm")
    my_part = lax.axis_index("tm")
    block_count = 1
    block_width = local_samples // block_count
    tiles_by_k = jnp.transpose(tiles, (0, 2, 1, 3, 4))
    columns_by_k = jnp.transpose(columns, (0, 2, 1))
    noise_rows = noise.reshape(step_count, local_samples, tile_rows, tile_size).transpose(
        0, 2, 1, 3
    )
    scale_rows = scale.reshape(step_count, tile_rows, 1, tile_size)
    full_tiles, full_columns = (
        lax.all_gather(tiles_by_k, "space", axis=2, tiled=True),
        lax.all_gather(columns_by_k, "space", axis=2, tiled=True),
    )

    def step_operands(time_step):
        return (full_tiles[time_step], full_columns[time_step])

    def sweep(incoming):
        current = incoming
        produced = [None] * step_count
        for reverse_step in range(step_count):
            time_step = step_count - 1 - reverse_step
            step_tile, step_column = step_operands(time_step)
            mixed = jnp.zeros((tile_rows, block_width, tile_size), jnp.float32)
            for which in range(tile_count):
                picked = jnp.take(current, step_column[which], axis=0)
                mixed = mixed + jnp.einsum(
                    "rsj,rij->rsi", picked, step_tile[which], preferred_element_type=jnp.float32
                )
            noise_block = noise_rows[time_step]
            updated = scale_rows[time_step] * (noise_block.astype(jnp.float32) + mixed)
            current = updated.astype(jnp.bfloat16)
            produced[time_step] = current
        return (current, jnp.stack(produced))

    def section(section_index, loop_carry):
        front, result = loop_carry
        incoming = shifted(front, "tm", -1)
        block_index = section_index - (part_count - 1 - my_part)
        active = (block_index >= 0) & (block_index < block_count)
        row_start = jnp.clip(block_index, 0, block_count - 1) * block_width
        first_field, block_out = sweep(incoming)
        chosen = jnp.where(active, block_out, result)
        new_result = lax.dynamic_update_slice_in_dim(result, chosen, row_start, 2)
        new_front = jnp.where(active, first_field, front)
        return (new_front, new_result)

    start_front = jnp.zeros((tile_rows, block_width, tile_size), jnp.bfloat16)
    start_result = jnp.zeros((step_count, tile_rows, local_samples, tile_size), jnp.bfloat16)
    _, result = lax.fori_loop(0, part_count + block_count - 1, section, (start_front, start_result))
    return result.transpose(0, 2, 1, 3).reshape(step_count, local_samples, node_count)


def solution(mesh):
    placed = (
        P("tm", "space", None),
        P("tm", None),
        P("tm", "space", None, None, None),
        P("tm", "space", None),
    )
    return jax.shard_map(
        on_device, mesh=mesh, in_specs=placed, out_specs=P("tm", "space", None), check_vma=False
    )
```

profile of v0, /device:TPU:1, one launch (start us, length us, event | category | flops | bytes accessed | tf_op | source)
XLA Modules:
  0.0 834.2 jit_solution(8011077418723320846)
XLA Ops:
  13.7 4.7 copy.14
  18.6 21.3 %all_gather.6 = s32[4,3,64]{1,0,2:T(4,128)S(1)} all-gather(s32[4,3,4]{1,0,2:T(4,128)S(1)} %bitcast.179), channel_id=1, replica_groups=mesh['tm'=8,'space'=16] {'space'}, dimensions={2}, use_global_device_ids=true | all-gather | bytes 3264 | tf_op jit(solution)/shard_map/all_gather | solution.py:32
  40.0 127.4 %all-gather.2.cloned.1.call-done = bf16[4,3,64,128,128]{4,3,2,1,0:T(8,128)(2,1)} async-done(((bf16[4,3,4,128,128]{4,3,2,1,0:T(8,128)(2,1)}), bf16[4,3,64,128,128]{4,3,2,1,0:T(8,128)(2,1)}) %all-gather.2.cloned.1.call-update) | async-done | bytes 25165840 | tf_op jit(solution)/shard_map/all_gather | solution.py:31
  167.4 655.0 %while.18 = (s32[]{:T(128)}, bf16[64,64,128]{2,1,0:T(8,128)(2,1)}, bf16[4,64,64,128]{3,2,1,0:T(8,128)(2,1)}, s32[]{:T(128)}, f32[4,64,1,128]{3,1,2,0:T(8,128)S(1...) while((s32[]{:T(128)}, bf16[64,64,128]{2,1,0:T(8,128)(2,1)}, ...), condition=%wide.region_1.0_spmd.clone, body=%wide.region_0.2_spmd.clone.sunk | while | flops 1641038336 | bytes 185005984 | solution.py:70
  170.2 13.5 %collective-permute-done = bf16[64,64,128]{2,1,0:T(8,128)(2,1)S(1)} collective-permute-done((bf16[64,64,128]{2,1,0:T(8,128)(2,1)S(1)}, bf16[64,64,128]{2,1,0:T(8,128)(2,1)S(1)}, u32[]{:S(2)}, u32[]{:S(2)}) %collective-permute-start) | collective-permute-done | bytes 1048608 | tf_op jit(solution)/shard_map/while/body/eval_jaxpr/ppermute | solution.py:10
  190.6 4.8 fusion.158
  240.5 4.6 broadcast_select_fusion.5
  251.7 14.0 %collective-permute-done = bf16[64,64,128]{2,1,0:T(8,128)(2,1)S(1)} collective-permute-done((bf16[64,64,128]{2,1,0:T(8,128)(2,1)S(1)}, bf16[64,64,128]{2,1,0:T(8,128)(2,1)S(1)}, u32[]{:S(2)}, u32[]{:S(2)}) %collective-permute-start) | collective-permute-done | bytes 1048608 | tf_op jit(solution)/shard_map/while/body/eval_jaxpr/ppermute | solution.py:10
  272.6 4.8 fusion.158
  279.0 4.3 fusion.160
  322.6 4.6 broadcast_select_fusion.5
  333.7 14.0 %collective-permute-done = bf16[64,64,128]{2,1,0:T(8,128)(2,1)S(1)} collective-permute-done((bf16[64,64,128]{2,1,0:T(8,128)(2,1)S(1)}, bf16[64,64,128]{2,1,0:T(8,128)(2,1)S(1)}, u32[]{:S(2)}, u32[]{:S(2)}) %collective-permute-start) | collective-permute-done | bytes 1048608 | tf_op jit(solution)/shard_map/while/body/eval_jaxpr/ppermute | solution.py:10
  354.6 4.8 fusion.158
  361.1 4.3 fusion.160
  404.6 4.6 broadcast_select_fusion.5
  415.7 14.0 %collective-permute-done = bf16[64,64,128]{2,1,0:T(8,128)(2,1)S(1)} collective-permute-done((bf16[64,64,128]{2,1,0:T(8,128)(2,1)S(1)}, bf16[64,64,128]{2,1,0:T(8,128)(2,1)S(1)}, u32[]{:S(2)}, u32[]{:S(2)}) %collective-permute-start) | collective-permute-done | bytes 1048608 | tf_op jit(solution)/shard_map/while/body/eval_jaxpr/ppermute | solution.py:10
  436.6 4.8 fusion.158
  486.6 4.6 broadcast_select_fusion.5
  497.8 14.0 %collective-permute-done = bf16[64,64,128]{2,1,0:T(8,128)(2,1)S(1)} collective-permute-done((bf16[64,64,128]{2,1,0:T(8,128)(2,1)S(1)}, bf16[64,64,128]{2,1,0:T(8,128)(2,1)S(1)}, u32[]{:S(2)}, u32[]{:S(2)}) %collective-permute-start) | collective-permute-done | bytes 1048608 | tf_op jit(solution)/shard_map/while/body/eval_jaxpr/ppermute | solution.py:10
  518.7 4.8 fusion.158
  525.1 4.3 fusion.160
  568.6 4.6 broadcast_select_fusion.5
  579.8 14.0 %collective-permute-done = bf16[64,64,128]{2,1,0:T(8,128)(2,1)S(1)} collective-permute-done((bf16[64,64,128]{2,1,0:T(8,128)(2,1)S(1)}, bf16[64,64,128]{2,1,0:T(8,128)(2,1)S(1)}, u32[]{:S(2)}, u32[]{:S(2)}) %collective-permute-start) | collective-permute-done | bytes 1048608 | tf_op jit(solution)/shard_map/while/body/eval_jaxpr/ppermute | solution.py:10
  600.7 4.8 fusion.158
  650.6 4.6 broadcast_select_fusion.5
  661.8 14.0 %collective-permute-done = bf16[64,64,128]{2,1,0:T(8,128)(2,1)S(1)} collective-permute-done((bf16[64,64,128]{2,1,0:T(8,128)(2,1)S(1)}, bf16[64,64,128]{2,1,0:T(8,128)(2,1)S(1)}, u32[]{:S(2)}, u32[]{:S(2)}) %collective-permute-start) | collective-permute-done | bytes 1048608 | tf_op jit(solution)/shard_map/while/body/eval_jaxpr/ppermute | solution.py:10
  682.7 4.8 fusion.158
  732.7 4.6 broadcast_select_fusion.5
  743.8 14.0 %collective-permute-done = bf16[64,64,128]{2,1,0:T(8,128)(2,1)S(1)} collective-permute-done((bf16[64,64,128]{2,1,0:T(8,128)(2,1)S(1)}, bf16[64,64,128]{2,1,0:T(8,128)(2,1)S(1)}, u32[]{:S(2)}, u32[]{:S(2)}) %collective-permute-start) | collective-permute-done | bytes 1048608 | tf_op jit(solution)/shard_map/while/body/eval_jaxpr/ppermute | solution.py:10
  764.7 4.8 fusion.158
  814.7 4.6 broadcast_select_fusion.5
  822.5 4.9 copy_bitcast_fusion
  (403 shorter events, 460.2 us)
Async XLA Ops:
  6.5 160.9 %all-gather.2.cloned.1.call-start = ((), (), s32[]{:S(2)}) async-start(), calls=%async_computation | async-start | bytes 26738688 | tf_op jit(solution)/shard_map/all_gather | solution.py:31
  13.7 4.7 copy-start.9
  13.7 26.2 %copy-start.8 = (f32[4,8192]{1,0:T(4,128)S(1)}, f32[4,8192]{1,0:T(4,128)}, u32[]{:S(2)}) copy-start(f32[4,8192]{1,0:T(4,128)} %param.9) | copy-start | bytes 393220
  167.5 17.9 %copy-start.2 = (bf16[64,64,128]{2,1,0:T(8,128)(2,1)}, bf16[64,64,128]{2,1,0:T(8,128)(2,1)S(1)}, u32[]{:S(2)}) copy-start(bf16[64,64,128]{2,1,0:T(8,128)(2,1)S(1)} %broadcast_select_fusion.4) | copy-start | bytes 3145732 | tf_op jit(solution)/shard_map/while
  167.5 16.2 %collective-permute-start = (bf16[64,64,128]{2,1,0:T(8,128)(2,1)S(1)}, bf16[64,64,128]{2,1,0:T(8,128)(2,1)S(1)}, u32[]{:S(2)}, u32[]{:S(2)}) collective-permute-start(bf16[64,64,128]{2,1,0:T(8,128)(2,1)S(1)} %broadcast_select_fusion.4), channel_id=1, source_target_pairs={{16,0},{32,16},{48,32},{64,48},{80,64},{96,80},{112,96},{17,1},{33... | collective-permute-start | bytes 3145736 | tf_op jit(solution)/shard_map/while/body/eval_jaxpr/ppermute | solution.py:10
  240.5 4.6 copy-start
  249.6 17.8 %copy-start.2 = (bf16[64,64,128]{2,1,0:T(8,128)(2,1)}, bf16[64,64,128]{2,1,0:T(8,128)(2,1)S(1)}, u32[]{:S(2)}) copy-start(bf16[64,64,128]{2,1,0:T(8,128)(2,1)S(1)} %broadcast_select_fusion.4) | copy-start | bytes 3145732 | tf_op jit(solution)/shard_map/while
  249.6 16.1 %collective-permute-start = (bf16[64,64,128]{2,1,0:T(8,128)(2,1)S(1)}, bf16[64,64,128]{2,1,0:T(8,128)(2,1)S(1)}, u32[]{:S(2)}, u32[]{:S(2)}) collective-permute-start(bf16[64,64,128]{2,1,0:T(8,128)(2,1)S(1)} %broadcast_select_fusion.4), channel_id=1, source_target_pairs={{16,0},{32,16},{48,32},{64,48},{80,64},{96,80},{112,96},{17,1},{33... | collective-permute-start | bytes 3145736 | tf_op jit(solution)/shard_map/while/body/eval_jaxpr/ppermute | solution.py:10
  315.7 3.5 copy-start.7
  322.5 4.6 copy-start
  331.6 17.8 %copy-start.2 = (bf16[64,64,128]{2,1,0:T(8,128)(2,1)}, bf16[64,64,128]{2,1,0:T(8,128)(2,1)S(1)}, u32[]{:S(2)}) copy-start(bf16[64,64,128]{2,1,0:T(8,128)(2,1)S(1)} %broadcast_select_fusion.4) | copy-start | bytes 3145732 | tf_op jit(solution)/shard_map/while
  331.6 16.1 %collective-permute-start = (bf16[64,64,128]{2,1,0:T(8,128)(2,1)S(1)}, bf16[64,64,128]{2,1,0:T(8,128)(2,1)S(1)}, u32[]{:S(2)}, u32[]{:S(2)}) collective-permute-start(bf16[64,64,128]{2,1,0:T(8,128)(2,1)S(1)} %broadcast_select_fusion.4), channel_id=1, source_target_pairs={{16,0},{32,16},{48,32},{64,48},{80,64},{96,80},{112,96},{17,1},{33... | collective-permute-start | bytes 3145736 | tf_op jit(solution)/shard_map/while/body/eval_jaxpr/ppermute | solution.py:10
  397.7 3.5 copy-start.7
  404.6 4.6 copy-start
  413.6 17.8 %copy-start.2 = (bf16[64,64,128]{2,1,0:T(8,128)(2,1)}, bf16[64,64,128]{2,1,0:T(8,128)(2,1)S(1)}, u32[]{:S(2)}) copy-start(bf16[64,64,128]{2,1,0:T(8,128)(2,1)S(1)} %broadcast_select_fusion.4) | copy-start | bytes 3145732 | tf_op jit(solution)/shard_map/while
  413.7 16.1 %collective-permute-start = (bf16[64,64,128]{2,1,0:T(8,128)(2,1)S(1)}, bf16[64,64,128]{2,1,0:T(8,128)(2,1)S(1)}, u32[]{:S(2)}, u32[]{:S(2)}) collective-permute-start(bf16[64,64,128]{2,1,0:T(8,128)(2,1)S(1)} %broadcast_select_fusion.4), channel_id=1, source_target_pairs={{16,0},{32,16},{48,32},{64,48},{80,64},{96,80},{112,96},{17,1},{33... | collective-permute-start | bytes 3145736 | tf_op jit(solution)/shard_map/while/body/eval_jaxpr/ppermute | solution.py:10
  479.7 3.5 copy-start.7
  486.6 4.6 copy-start
  495.7 17.8 %copy-start.2 = (bf16[64,64,128]{2,1,0:T(8,128)(2,1)}, bf16[64,64,128]{2,1,0:T(8,128)(2,1)S(1)}, u32[]{:S(2)}) copy-start(bf16[64,64,128]{2,1,0:T(8,128)(2,1)S(1)} %broadcast_select_fusion.4) | copy-start | bytes 3145732 | tf_op jit(solution)/shard_map/while
  495.7 16.1 %collective-permute-start = (bf16[64,64,128]{2,1,0:T(8,128)(2,1)S(1)}, bf16[64,64,128]{2,1,0:T(8,128)(2,1)S(1)}, u32[]{:S(2)}, u32[]{:S(2)}) collective-permute-start(bf16[64,64,128]{2,1,0:T(8,128)(2,1)S(1)} %broadcast_select_fusion.4), channel_id=1, source_target_pairs={{16,0},{32,16},{48,32},{64,48},{80,64},{96,80},{112,96},{17,1},{33... | collective-permute-start | bytes 3145736 | tf_op jit(solution)/shard_map/while/body/eval_jaxpr/ppermute | solution.py:10
  568.6 4.6 copy-start
  577.7 17.8 %copy-start.2 = (bf16[64,64,128]{2,1,0:T(8,128)(2,1)}, bf16[64,64,128]{2,1,0:T(8,128)(2,1)S(1)}, u32[]{:S(2)}) copy-start(bf16[64,64,128]{2,1,0:T(8,128)(2,1)S(1)} %broadcast_select_fusion.4) | copy-start | bytes 3145732 | tf_op jit(solution)/shard_map/while
  577.7 16.1 %collective-permute-start = (bf16[64,64,128]{2,1,0:T(8,128)(2,1)S(1)}, bf16[64,64,128]{2,1,0:T(8,128)(2,1)S(1)}, u32[]{:S(2)}, u32[]{:S(2)}) collective-permute-start(bf16[64,64,128]{2,1,0:T(8,128)(2,1)S(1)} %broadcast_select_fusion.4), channel_id=1, source_target_pairs={{16,0},{32,16},{48,32},{64,48},{80,64},{96,80},{112,96},{17,1},{33... | collective-permute-start | bytes 3145736 | tf_op jit(solution)/shard_map/while/body/eval_jaxpr/ppermute | solution.py:10
  643.8 3.5 copy-start.7
  650.6 4.6 copy-start
  659.7 17.8 %copy-start.2 = (bf16[64,64,128]{2,1,0:T(8,128)(2,1)}, bf16[64,64,128]{2,1,0:T(8,128)(2,1)S(1)}, u32[]{:S(2)}) copy-start(bf16[64,64,128]{2,1,0:T(8,128)(2,1)S(1)} %broadcast_select_fusion.4) | copy-start | bytes 3145732 | tf_op jit(solution)/shard_map/while
  659.7 16.1 %collective-permute-start = (bf16[64,64,128]{2,1,0:T(8,128)(2,1)S(1)}, bf16[64,64,128]{2,1,0:T(8,128)(2,1)S(1)}, u32[]{:S(2)}, u32[]{:S(2)}) collective-permute-start(bf16[64,64,128]{2,1,0:T(8,128)(2,1)S(1)} %broadcast_select_fusion.4), channel_id=1, source_target_pairs={{16,0},{32,16},{48,32},{64,48},{80,64},{96,80},{112,96},{17,1},{33... | collective-permute-start | bytes 3145736 | tf_op jit(solution)/shard_map/while/body/eval_jaxpr/ppermute | solution.py:10
  725.8 3.5 copy-start.7
  732.6 4.6 copy-start
  741.7 17.8 %copy-start.2 = (bf16[64,64,128]{2,1,0:T(8,128)(2,1)}, bf16[64,64,128]{2,1,0:T(8,128)(2,1)S(1)}, u32[]{:S(2)}) copy-start(bf16[64,64,128]{2,1,0:T(8,128)(2,1)S(1)} %broadcast_select_fusion.4) | copy-start | bytes 3145732 | tf_op jit(solution)/shard_map/while
  741.7 16.1 %collective-permute-start = (bf16[64,64,128]{2,1,0:T(8,128)(2,1)S(1)}, bf16[64,64,128]{2,1,0:T(8,128)(2,1)S(1)}, u32[]{:S(2)}, u32[]{:S(2)}) collective-permute-start(bf16[64,64,128]{2,1,0:T(8,128)(2,1)S(1)} %broadcast_select_fusion.4), channel_id=1, source_target_pairs={{16,0},{32,16},{48,32},{64,48},{80,64},{96,80},{112,96},{17,1},{33... | collective-permute-start | bytes 3145736 | tf_op jit(solution)/shard_map/while/body/eval_jaxpr/ppermute | solution.py:10
  814.7 4.6 copy-start
  (43 other events, 130.9 us)
Sparse Core Ops, SparseCore 0:
  9.5 157.8 all-gather.1
where the time goes:
time: 836 us; the launch traced here: 834 us
  matrix products  350 us (42%)
  waiting for transfers between devices  239 us (29%)
  local copies, waits for them, and re-layouts  173 us (21%)
  blocking collectives  21.3 us (3%)
  other arithmetic  18.9 us (2%)
  starting transfers between devices  16 us (2%)
  between operations  13.5 us (2%)
    dot_general x96, matrix products, sweep(): jnp.einsum('rsj,rij->rsi', picked, step_tile[which], preferred_element_ty...  350 us
    gather x96, local copies, waits for them, and re-layouts, sweep(): picked = jnp.take(current, step_column[which], axis=0)  140 us
    all_gather x1, waiting for transfers between devices, on_device(): lax.all_gather(tiles_by_k, 'space', axis=2, tiled=True)  127 us
    ppermute x8, waiting for transfers between devices, shifted(): return lax.ppermute(shard, axis, pairs)  112 us
    all_gather x1, blocking collectives, on_device(): lax.all_gather(columns_by_k, 'space', axis=2, tiled=True)  21.3 us
  transfers between devices with their start and end apart: 9, of which 9 were waited for; matrix products, arithmetic and copies ran while one was open for 1% of the time, Pallas kernels for 0%

commit v1 on v0

--- a/solution.py
+++ b/solution.py
@@ -27,8 +27,20 @@
         0, 2, 1, 3
     )
     scale_rows = scale.reshape(step_count, tile_rows, 1, tile_size)
+
+    def step_on_region(local_block, peer_axis):
+        return jnp.concatenate(
+            lax.all_to_all(
+                jnp.stack(tuple((local_block for _ in range(lax.psum(1, peer_axis)))), axis=0),
+                peer_axis,
+                0,
+                0,
+            ),
+            axis=2,
+        )
+
     full_tiles, full_columns = (
-        lax.all_gather(tiles_by_k, "space", axis=2, tiled=True),
+        step_on_region(tiles_by_k, "space"),
         lax.all_gather(columns_by_k, "space", axis=2, tiled=True),
     )
 

time: 836 us -> 1090 us (1.30)
  blocking collectives: 21.3 us -> 375 us
  waiting for transfers between devices: 239 us -> 112 us
  local copies, waits for them, and re-layouts: 173 us -> 203 us
  between operations: 13.5 us -> 0.09 us
  starting transfers between devices: 16 us -> 28.7 us
    all_gather x1, blocking collectives: 21.3 us -> 375 us  [on_device(): lax.all_gather(columns_by_k, 'space', axis=2, tiled=True)]
    all_gather x1 -> x0, waiting for transfers between devices: 127 us -> none  [on_device(): lax.all_gather(tiles_by_k, 'space', axis=2, tiled=True)]
    all_to_all x0 -> x1, local copies, waits for them, and re-layouts: none -> 21.1 us  [step_on_region(): lax.all_to_all(jnp.stack(tuple((local_block for _ in range(lax.psum(1, pe...]
  transfers between devices with their start and end apart: 9 -> 9, of which waited for: 9 -> 8; matrix products, arithmetic and copies ran while one was open for 1% -> 1% of each run, Pallas kernels for 0% -> 0%
where the time goes in v1:
time: 1090 us
  blocking collectives  375 us (34%)
  matrix products  351 us (32%)
  local copies, waits for them, and re-layouts  203 us (19%)
  waiting for transfers between devices  112 us (10%)
  starting transfers between devices  28.7 us (3%)
  other arithmetic  18.9 us (2%)
    all_gather x1, blocking collectives, on_device(): lax.all_gather(columns_by_k, 'space', axis=2, tiled=True)  375 us
    dot_general x96, matrix products, sweep(): jnp.einsum('rsj,rij->rsi', picked, step_tile[which], preferred_element_ty...  351 us
    gather x96, local copies, waits for them, and re-layouts, sweep(): picked = jnp.take(current, step_column[which], axis=0)  140 us
    ppermute x8, waiting for transfers between devices, shifted(): return lax.ppermute(shard, axis, pairs)  112 us
  transfers between devices with their start and end apart: 9, of which 8 were waited for; matrix products, arithmetic and copies ran while one was open for 1% of the time, Pallas kernels for 0%

profile of v1, /device:TPU:1, one launch (start us, length us, event | category | flops | bytes accessed | tf_op | source)
XLA Modules:
  0.0 1090.7 jit_solution(4680546593511911621)
XLA Ops:
  1.5 9.0 stack.64
  10.5 7.6 all-to-all-start
  22.6 4.7 copy.20
  27.4 374.8 %all_gather.3 = s32[4,3,64]{1,0,2:T(4,128)S(1)} all-gather(s32[4,3,4]{1,0,2:T(4,128)S(1)} %bitcast.181), channel_id=1, replica_groups=mesh['tm'=8,'space'=16] {'space'}, dimensions={2}, use_global_device_ids=true | all-gather | bytes 3264 | tf_op jit(solution)/shard_map/all_gather | solution.py:44
  402.3 21.1 %copy.19 = bf16[16,4,3,4,128,128]{5,4,3,0,2,1:T(8,128)(2,1)} copy(bf16[16,4,3,4,128,128]{5,4,3,2,1,0:T(8,128)(2,1)} %all-to-all-done) | data formatting | bytes 50331648 | tf_op jit(solution)/shard_map/all_to_all | solution.py:33
  423.4 662.5 %while.18 = (s32[]{:T(128)}, bf16[64,64,128]{2,1,0:T(8,128)(2,1)}, bf16[4,64,64,128]{3,2,1,0:T(8,128)(2,1)}, s32[]{:T(128)}, f32[4,64,1,128]{3,1,2,0:T(8,128)S(1...) while((s32[]{:T(128)}, bf16[64,64,128]{2,1,0:T(8,128)(2,1)}, ...), condition=%wide.region_1.0_spmd.clone, body=%wide.region_0.2_spmd.clone.sunk | while | flops 1641038336 | bytes 185005984 | solution.py:82
  423.5 7.6 collective-permute-start
  431.2 13.8 %collective-permute-done = bf16[64,64,128]{2,1,0:T(8,128)(2,1)S(1)} collective-permute-done((bf16[64,64,128]{2,1,0:T(8,128)(2,1)S(1)}, bf16[64,64,128]{2,1,0:T(8,128)(2,1)S(1)}, u32[]{:S(2)}, u32[]{:S(2)}) %collective-permute-start) | collective-permute-done | bytes 1048608 | tf_op jit(solution)/shard_map/while/body/eval_jaxpr/ppermute | solution.py:10
  451.9 4.8 fusion.158
  502.0 4.7 broadcast_select_fusion.5
  513.3 14.0 %collective-permute-done = bf16[64,64,128]{2,1,0:T(8,128)(2,1)S(1)} collective-permute-done((bf16[64,64,128]{2,1,0:T(8,128)(2,1)S(1)}, bf16[64,64,128]{2,1,0:T(8,128)(2,1)S(1)}, u32[]{:S(2)}, u32[]{:S(2)}) %collective-permute-start) | collective-permute-done | bytes 1048608 | tf_op jit(solution)/shard_map/while/body/eval_jaxpr/ppermute | solution.py:10
  534.2 4.8 fusion.158
  584.3 4.7 broadcast_select_fusion.5
  595.6 14.0 %collective-permute-done = bf16[64,64,128]{2,1,0:T(8,128)(2,1)S(1)} collective-permute-done((bf16[64,64,128]{2,1,0:T(8,128)(2,1)S(1)}, bf16[64,64,128]{2,1,0:T(8,128)(2,1)S(1)}, u32[]{:S(2)}, u32[]{:S(2)}) %collective-permute-start) | collective-permute-done | bytes 1048608 | tf_op jit(solution)/shard_map/while/body/eval_jaxpr/ppermute | solution.py:10
  616.5 4.8 fusion.158
  666.6 4.7 broadcast_select_fusion.5
  677.9 14.0 %collective-permute-done = bf16[64,64,128]{2,1,0:T(8,128)(2,1)S(1)} collective-permute-done((bf16[64,64,128]{2,1,0:T(8,128)(2,1)S(1)}, bf16[64,64,128]{2,1,0:T(8,128)(2,1)S(1)}, u32[]{:S(2)}, u32[]{:S(2)}) %collective-permute-start) | collective-permute-done | bytes 1048608 | tf_op jit(solution)/shard_map/while/body/eval_jaxpr/ppermute | solution.py:10
  698.8 4.8 fusion.158
  748.9 4.7 broadcast_select_fusion.5
  760.1 14.0 %collective-permute-done = bf16[64,64,128]{2,1,0:T(8,128)(2,1)S(1)} collective-permute-done((bf16[64,64,128]{2,1,0:T(8,128)(2,1)S(1)}, bf16[64,64,128]{2,1,0:T(8,128)(2,1)S(1)}, u32[]{:S(2)}, u32[]{:S(2)}) %collective-permute-start) | collective-permute-done | bytes 1048608 | tf_op jit(solution)/shard_map/while/body/eval_jaxpr/ppermute | solution.py:10
  781.1 4.8 fusion.158
  831.1 4.7 broadcast_select_fusion.5
  842.4 14.0 %collective-permute-done = bf16[64,64,128]{2,1,0:T(8,128)(2,1)S(1)} collective-permute-done((bf16[64,64,128]{2,1,0:T(8,128)(2,1)S(1)}, bf16[64,64,128]{2,1,0:T(8,128)(2,1)S(1)}, u32[]{:S(2)}, u32[]{:S(2)}) %collective-permute-start) | collective-permute-done | bytes 1048608 | tf_op jit(solution)/shard_map/while/body/eval_jaxpr/ppermute | solution.py:10
  863.3 4.8 fusion.158
  913.4 4.7 broadcast_select_fusion.5
  924.7 14.0 %collective-permute-done = bf16[64,64,128]{2,1,0:T(8,128)(2,1)S(1)} collective-permute-done((bf16[64,64,128]{2,1,0:T(8,128)(2,1)S(1)}, bf16[64,64,128]{2,1,0:T(8,128)(2,1)S(1)}, u32[]{:S(2)}, u32[]{:S(2)}) %collective-permute-start) | collective-permute-done | bytes 1048608 | tf_op jit(solution)/shard_map/while/body/eval_jaxpr/ppermute | solution.py:10
  945.6 4.8 fusion.158
  995.7 4.7 broadcast_select_fusion.5
  1007.0 14.0 %collective-permute-done = bf16[64,64,128]{2,1,0:T(8,128)(2,1)S(1)} collective-permute-done((bf16[64,64,128]{2,1,0:T(8,128)(2,1)S(1)}, bf16[64,64,128]{2,1,0:T(8,128)(2,1)S(1)}, u32[]{:S(2)}, u32[]{:S(2)}) %collective-permute-start) | collective-permute-done | bytes 1048608 | tf_op jit(solution)/shard_map/while/body/eval_jaxpr/ppermute | solution.py:10
  1027.9 4.8 fusion.158
  1078.0 4.7 broadcast_select_fusion.5
  1085.9 4.9 copy_bitcast_fusion
  (404 shorter events, 470.7 us)
Async XLA Ops:
  10.5 391.8 %all-to-all-start = ((bf16[16,4,3,4,128,128]{5,4,3,2,1,0:T(8,128)(2,1)}), bf16[16,4,3,4,128,128]{5,4,3,2,1,0:T(8,128)(2,1)}, u32[]{:S(2)}, u32[]{:S(2)}) async-start(bf16[16,4,3,4,128,128]{5,4,3,2,1,0:T(8,128)(2,1)} %stack.64), calls=%async_computation | async-start | bytes 50331648 | tf_op jit(solution)/shard_map/all_to_all | solution.py:33
  22.5 4.7 copy-start.9
  22.6 379.7 %copy-start.8 = (f32[4,8192]{1,0:T(4,128)S(1)}, f32[4,8192]{1,0:T(4,128)}, u32[]{:S(2)}) copy-start(f32[4,8192]{1,0:T(4,128)} %param.9) | copy-start | bytes 393220
  423.5 23.3 %copy-start.2 = (bf16[64,64,128]{2,1,0:T(8,128)(2,1)}, bf16[64,64,128]{2,1,0:T(8,128)(2,1)S(1)}, u32[]{:S(2)}) copy-start(bf16[64,64,128]{2,1,0:T(8,128)(2,1)S(1)} %broadcast_select_fusion.4) | copy-start | bytes 3145732 | tf_op jit(solution)/shard_map/while
  423.5 21.6 %collective-permute-start = (bf16[64,64,128]{2,1,0:T(8,128)(2,1)S(1)}, bf16[64,64,128]{2,1,0:T(8,128)(2,1)S(1)}, u32[]{:S(2)}, u32[]{:S(2)}) collective-permute-start(bf16[64,64,128]{2,1,0:T(8,128)(2,1)S(1)} %broadcast_select_fusion.4), channel_id=1, source_target_pairs={{16,0},{32,16},{48,32},{64,48},{80,64},{96,80},{112,96},{17,1},{33... | collective-permute-start | bytes 3145736 | tf_op jit(solution)/shard_map/while/body/eval_jaxpr/ppermute | solution.py:10
  495.1 3.5 copy-start.7
  502.0 4.7 copy-start
  511.2 17.9 %copy-start.2 = (bf16[64,64,128]{2,1,0:T(8,128)(2,1)}, bf16[64,64,128]{2,1,0:T(8,128)(2,1)S(1)}, u32[]{:S(2)}) copy-start(bf16[64,64,128]{2,1,0:T(8,128)(2,1)S(1)} %broadcast_select_fusion.4) | copy-start | bytes 3145732 | tf_op jit(solution)/shard_map/while
  511.2 16.1 %collective-permute-start = (bf16[64,64,128]{2,1,0:T(8,128)(2,1)S(1)}, bf16[64,64,128]{2,1,0:T(8,128)(2,1)S(1)}, u32[]{:S(2)}, u32[]{:S(2)}) collective-permute-start(bf16[64,64,128]{2,1,0:T(8,128)(2,1)S(1)} %broadcast_select_fusion.4), channel_id=1, source_target_pairs={{16,0},{32,16},{48,32},{64,48},{80,64},{96,80},{112,96},{17,1},{33... | collective-permute-start | bytes 3145736 | tf_op jit(solution)/shard_map/while/body/eval_jaxpr/ppermute | solution.py:10
  577.4 3.5 copy-start.7
  584.3 4.7 copy-start
  593.5 17.9 %copy-start.2 = (bf16[64,64,128]{2,1,0:T(8,128)(2,1)}, bf16[64,64,128]{2,1,0:T(8,128)(2,1)S(1)}, u32[]{:S(2)}) copy-start(bf16[64,64,128]{2,1,0:T(8,128)(2,1)S(1)} %broadcast_select_fusion.4) | copy-start | bytes 3145732 | tf_op jit(solution)/shard_map/while
  593.5 16.1 %collective-permute-start = (bf16[64,64,128]{2,1,0:T(8,128)(2,1)S(1)}, bf16[64,64,128]{2,1,0:T(8,128)(2,1)S(1)}, u32[]{:S(2)}, u32[]{:S(2)}) collective-permute-start(bf16[64,64,128]{2,1,0:T(8,128)(2,1)S(1)} %broadcast_select_fusion.4), channel_id=1, source_target_pairs={{16,0},{32,16},{48,32},{64,48},{80,64},{96,80},{112,96},{17,1},{33... | collective-permute-start | bytes 3145736 | tf_op jit(solution)/shard_map/while/body/eval_jaxpr/ppermute | solution.py:10
  659.7 3.5 copy-start.7
  666.6 4.7 copy-start
  675.8 17.9 %copy-start.2 = (bf16[64,64,128]{2,1,0:T(8,128)(2,1)}, bf16[64,64,128]{2,1,0:T(8,128)(2,1)S(1)}, u32[]{:S(2)}) copy-start(bf16[64,64,128]{2,1,0:T(8,128)(2,1)S(1)} %broadcast_select_fusion.4) | copy-start | bytes 3145732 | tf_op jit(solution)/shard_map/while
  675.8 16.1 %collective-permute-start = (bf16[64,64,128]{2,1,0:T(8,128)(2,1)S(1)}, bf16[64,64,128]{2,1,0:T(8,128)(2,1)S(1)}, u32[]{:S(2)}, u32[]{:S(2)}) collective-permute-start(bf16[64,64,128]{2,1,0:T(8,128)(2,1)S(1)} %broadcast_select_fusion.4), channel_id=1, source_target_pairs={{16,0},{32,16},{48,32},{64,48},{80,64},{96,80},{112,96},{17,1},{33... | collective-permute-start | bytes 3145736 | tf_op jit(solution)/shard_map/while/body/eval_jaxpr/ppermute | solution.py:10
  742.0 3.5 copy-start.7
  748.8 4.7 copy-start
  758.1 17.9 %copy-start.2 = (bf16[64,64,128]{2,1,0:T(8,128)(2,1)}, bf16[64,64,128]{2,1,0:T(8,128)(2,1)S(1)}, u32[]{:S(2)}) copy-start(bf16[64,64,128]{2,1,0:T(8,128)(2,1)S(1)} %broadcast_select_fusion.4) | copy-start | bytes 3145732 | tf_op jit(solution)/shard_map/while
  758.1 16.1 %collective-permute-start = (bf16[64,64,128]{2,1,0:T(8,128)(2,1)S(1)}, bf16[64,64,128]{2,1,0:T(8,128)(2,1)S(1)}, u32[]{:S(2)}, u32[]{:S(2)}) collective-permute-start(bf16[64,64,128]{2,1,0:T(8,128)(2,1)S(1)} %broadcast_select_fusion.4), channel_id=1, source_target_pairs={{16,0},{32,16},{48,32},{64,48},{80,64},{96,80},{112,96},{17,1},{33... | collective-permute-start | bytes 3145736 | tf_op jit(solution)/shard_map/while/body/eval_jaxpr/ppermute | solution.py:10
  831.1 4.7 copy-start
  840.3 17.9 %copy-start.2 = (bf16[64,64,128]{2,1,0:T(8,128)(2,1)}, bf16[64,64,128]{2,1,0:T(8,128)(2,1)S(1)}, u32[]{:S(2)}) copy-start(bf16[64,64,128]{2,1,0:T(8,128)(2,1)S(1)} %broadcast_select_fusion.4) | copy-start | bytes 3145732 | tf_op jit(solution)/shard_map/while
  840.4 16.1 %collective-permute-start = (bf16[64,64,128]{2,1,0:T(8,128)(2,1)S(1)}, bf16[64,64,128]{2,1,0:T(8,128)(2,1)S(1)}, u32[]{:S(2)}, u32[]{:S(2)}) collective-permute-start(bf16[64,64,128]{2,1,0:T(8,128)(2,1)S(1)} %broadcast_select_fusion.4), channel_id=1, source_target_pairs={{16,0},{32,16},{48,32},{64,48},{80,64},{96,80},{112,96},{17,1},{33... | collective-permute-start | bytes 3145736 | tf_op jit(solution)/shard_map/while/body/eval_jaxpr/ppermute | solution.py:10
  913.4 4.7 copy-start
  922.6 17.9 %copy-start.2 = (bf16[64,64,128]{2,1,0:T(8,128)(2,1)}, bf16[64,64,128]{2,1,0:T(8,128)(2,1)S(1)}, u32[]{:S(2)}) copy-start(bf16[64,64,128]{2,1,0:T(8,128)(2,1)S(1)} %broadcast_select_fusion.4) | copy-start | bytes 3145732 | tf_op jit(solution)/shard_map/while
  922.6 16.1 %collective-permute-start = (bf16[64,64,128]{2,1,0:T(8,128)(2,1)S(1)}, bf16[64,64,128]{2,1,0:T(8,128)(2,1)S(1)}, u32[]{:S(2)}, u32[]{:S(2)}) collective-permute-start(bf16[64,64,128]{2,1,0:T(8,128)(2,1)S(1)} %broadcast_select_fusion.4), channel_id=1, source_target_pairs={{16,0},{32,16},{48,32},{64,48},{80,64},{96,80},{112,96},{17,1},{33... | collective-permute-start | bytes 3145736 | tf_op jit(solution)/shard_map/while/body/eval_jaxpr/ppermute | solution.py:10
  988.8 3.5 copy-start.7
  995.7 4.7 copy-start
  1004.9 17.9 %copy-start.2 = (bf16[64,64,128]{2,1,0:T(8,128)(2,1)}, bf16[64,64,128]{2,1,0:T(8,128)(2,1)S(1)}, u32[]{:S(2)}) copy-start(bf16[64,64,128]{2,1,0:T(8,128)(2,1)S(1)} %broadcast_select_fusion.4) | copy-start | bytes 3145732 | tf_op jit(solution)/shard_map/while
  1004.9 16.1 %collective-permute-start = (bf16[64,64,128]{2,1,0:T(8,128)(2,1)S(1)}, bf16[64,64,128]{2,1,0:T(8,128)(2,1)S(1)}, u32[]{:S(2)}, u32[]{:S(2)}) collective-permute-start(bf16[64,64,128]{2,1,0:T(8,128)(2,1)S(1)} %broadcast_select_fusion.4), channel_id=1, source_target_pairs={{16,0},{32,16},{48,32},{64,48},{80,64},{96,80},{112,96},{17,1},{33... | collective-permute-start | bytes 3145736 | tf_op jit(solution)/shard_map/while/body/eval_jaxpr/ppermute | solution.py:10
  1078.0 4.7 copy-start
  (43 other events, 131.6 us)
